TPU v7x, 512 devices: a whole 4x8x8 slice. The times are simulated.
512 devices in a mesh: section: 8 (over x, z_hi), dp: 64 (over y, z_lo, core).
Axes of the slice: x: 4, y: 8, z: 8 (z_hi: 2, z_lo: 4; z = z_hi * 4 + z_lo), core: 2. Of those that a mesh axis runs over, the one named last changes fastest.
Arguments:
- activations: bfloat16 [8, 32, 512], P('section'), may hold values from -6 to 6
- out_grads: bfloat16 [8, 512, 53248], P('section', None, 'dp'), may hold values from -16 to 16
- master: float32 [8, 32, 53248], P('section', None, 'dp'), may hold values from -3 to 3
- moment_one: float32 [8, 32, 53248], P('section', None, 'dp'), may hold values from -3 to 3
- moment_two: float32 [8, 32, 53248], P('section', None, 'dp'), may hold values from 0.25 to 4
Outputs:
- to_previous: bfloat16 [8, 512, 32], P('section', 'dp')
- new_master: float32 [8, 32, 53248], P('section', None, 'dp')
- new_moment_one: float32 [8, 32, 53248], P('section', None, 'dp')
- new_moment_two: float32 [8, 32, 53248], P('section', None, 'dp')
- new_weights: bfloat16 [8, 32, 53248], P('section')
All inputs are finite; a program needn't handle non-finite values.
Results may differ from a plain program's by a relative error of at most 0.0049.
Values may be sent and summed in bfloat16 or wider, within the bound.
A program may use at most 128 MiB of HBM per device.

v0:
```python
import math

import jax
import jax.numpy as jnp
from jax import lax
from jax.sharding import PartitionSpec as P

FF = 53248
SLAB = 32


def shifted(value, axis, by):
    size = lax.axis_size(axis)
    pairs = [(i, i + by) for i in range(size) if 0 <= i + by < size]
    return lax.ppermute(value, axis, pairs)


def body(activations, out_grads, master, moment_one, moment_two):
    weights = master.astype(jnp.bfloat16)
    grads_local = out_grads[0]
    acts_local = activations[0]
    all_rows = grads_local.shape[0]
    tok_share = all_rows // lax.axis_size("dp")
    summed = lax.psum(
        lax.dot_general(
            grads_local, weights[0], (((1,), (1,)), ((), ())), preferred_element_type=jnp.float32
        ),
        "dp",
    )
    offset = lax.axis_index("dp") * tok_share
    mine_input = lax.dynamic_slice_in_dim(summed, offset, tok_share, 0)
    input_grad = mine_input.astype(jnp.bfloat16)[None]
    to_previous = shifted(input_grad, "section", -1)
    grad = jnp.dot(acts_local, grads_local, preferred_element_type=jnp.float32)
    total = lax.psum(jnp.sum(grad * grad), ("section", "dp"))
    limit = math.sqrt(lax.axis_size("section") * FF * SLAB)
    clip = jnp.minimum(1.0, limit / jnp.sqrt(total + 1e-06))
    scaled = (clip * grad)[None]
    new_one = 0.9 * moment_one + 0.1 * scaled
    new_two = 0.95 * moment_two + 0.05 * scaled * scaled
    new_master = master - 0.05 * (new_one / (1.0 - 0.9**10)) / (
        jnp.sqrt(new_two / (1.0 - 0.95**10)) + 1e-08
    )
    new_weights = lax.all_gather(new_master.astype(jnp.bfloat16), "dp", axis=2, tiled=True)
    return (to_previous, new_master, new_one, new_two, new_weights)


def solution(mesh):
    placed = (
        P("section", None, None),
        P("section", None, "dp"),
        P("section", None, "dp"),
        P("section", None, "dp"),
        P("section", None, "dp"),
    )
    return jax.shard_map(
        body,
        mesh=mesh,
        in_specs=placed,
        out_specs=(
            P("section", "dp", None),
            P("section", None, "dp"),
            P("section", None, "dp"),
            P("section", None, "dp"),
            P("section", None, None),
        ),
        check_vma=False,
    )
```

profile of v0, /device:TPU:1, one launch (start us, length us, event | category | flops | bytes accessed | tf_op | source)
XLA Modules:
  0.0 450.4 jit_solution(1552384753438560625)
XLA Ops:
  7.2 0.0 copy-start
  7.2 0.0 all-gather.2.cloned.1.call-start
  7.2 1.1 copy-done
  8.3 1.7 multiply_reduce_fusion
  10.1 106.1 %psum.15 = f32[]{:T(128)} all-reduce(f32[]{:T(128)} %get-tuple-element.14), channel_id=1, replica_groups=mesh['section'=8,'dp'=64] {'section','dp'}, use_global_device_ids=true, to_apply=%region_2.0 | all-reduce | flops 1 | bytes 8 | tf_op jit(solution)/shard_map/psum | solution.py:35
  116.8 1.8 fusion.10
  118.6 1.0 copy.10
  119.6 0.0 all-gather.2.cloned.1.call-update
  119.7 1.3 fusion.2
  121.0 263.7 %psum.14 = bf16[512,32]{1,0:T(8,128)(2,1)S(1)} all-reduce(f32[512,32]{1,0:T(8,128)S(1)} %fusion.2), channel_id=1, replica_groups=mesh['section'=8,'dp'=64] {'dp'}, use_global_device_ids=true, to_apply=%region_0.0 | all-reduce | flops 16384 | bytes 98304 | tf_op jit(solution)/shard_map/psum | solution.py:24
  384.7 1.3 collective-permute-start
  386.0 6.9 %collective-permute-done = bf16[1,8,32]{2,1,0:T(8,128)(2,1)S(1)} collective-permute-done((bf16[1,8,32]{2,1,0:T(8,128)(2,1)S(1)}, bf16[1,8,32]{2,1,0:T(8,128)(2,1)S(1)}, u32[]{:S(2)}, u32[]{:S(2)}) %collective-permute-start) | collective-permute-done | bytes 544 | tf_op jit(solution)/shard_map/ppermute | solution.py:15
  393.0 0.0 all-gather.2.cloned.1.call-done
  393.0 50.0 %copy.11 = bf16[1,32,53248]{2,1,0:T(8,128)(2,1)} copy(bf16[1,32,53248]{1,0,2:T(2,128)(2,1)} %all-gather.2.cloned.1.call-done) | data formatting | bytes 6815744
  442.9 0.6 copy.13
  (1 shorter events, 0.0 us)
Async XLA Ops:
  7.2 1.2 copy-start
  7.2 385.8 %all-gather.2.cloned.1.call-start = ((), (), s32[]{:S(2)}) async-start(), calls=%async_computation | async-start | bytes 27688960 | tf_op jit(solution)/shard_map/all_gather | solution.py:44
  384.7 8.2 %collective-permute-start = (bf16[1,8,32]{2,1,0:T(8,128)(2,1)S(1)}, bf16[1,8,32]{2,1,0:T(8,128)(2,1)S(1)}, u32[]{:S(2)}, u32[]{:S(2)}) collective-permute-start(bf16[1,8,32]{2,1,0:T(8,128)(2,1)S(1)} %fusion.9), channel_id=1, source_target_pairs={{64,0},{128,64},{192,128},{256,192},{320,256},{384,320},{448,384},... | collective-permute-start | bytes 1544 | tf_op jit(solution)/shard_map/ppermute | solution.py:15
Sparse Core Ops, SparseCore 0:
  119.8 157.4 all-gather.1
where the time goes:
time: 457 us; the launch traced here: 450 us
  blocking collectives  370 us (81%)
  local copies, waits for them, and re-layouts  52.7 us (12%)
  between operations  14.8 us (3%)
  waiting for transfers between devices  6.95 us (2%)
    psum x1, blocking collectives, body(): lax.psum(lax.dot_general(grads_local, weights[0], (((1,), (1,)), ((), ())...  264 us
    psum x1, blocking collectives, body(): total = lax.psum(jnp.sum(grad * grad), ('section', 'dp'))  106 us
    unnamed x4, local copies, waits for them, and re-layouts  51.7 us
  transfers between devices with their start and end apart: 2, of which 1 were waited for; matrix products, arithmetic and copies ran while one was open for 0% of the time, Pallas kernels for 0%

commit v1 on v0

v1 whole, which is shorter than its diff:
```python
import functools
import math

import jax
import jax.numpy as jnp
from jax import lax
from jax.experimental import pallas as pl
from jax.experimental.pallas import tpu as pltpu
from jax.sharding import PartitionSpec as P

FF = 53248
SLAB = 32
MESH = pl.DeviceIdType.MESH

NX, NY, NZ, NZL = 4, 8, 8, 4
COLS = FF // 64
WIDE = 2 * COLS
HALF = SLAB // 2
CUT = 9 * 128
SPLIT_STEPS = 5
VMEM_GRANT = 63250000


def adam(master, grad, one, two, clip):
    scaled = clip * grad
    new_one = 0.9 * one + 0.1 * scaled
    new_two = 0.95 * two + 0.05 * scaled * scaled
    new_master = master - 0.05 * (new_one / (1.0 - 0.9**10)) / (
        jnp.sqrt(new_two / (1.0 - 0.95**10)) + 1e-08
    )
    return new_master, new_one, new_two


def main_kernel(
    acts_hbm, og_hbm, master_hbm, one_hbm, two_hbm,
    w_out, master_out, one_out, two_out, prev_out,
    acts, og, state, other, norms, parts_a, got_a, part_b, got_b,
    load_sem, norm_send, norm_recv, pair_send, pair_recv,
    a_send, a_recv, b_send, b_recv,
    ring_full_send, ring_cut_send, ring_recv,
    core_send, core_recv, z_full_send, z_cut_send, z_full_recv, z_cut_recv,
):
    s = lax.axis_index("section")
    d = lax.axis_index("dp")
    x, zh = s // 2, s % 2
    y, zl, c = d // 8, (d // 2) % 4, d % 2
    z = zh * NZL + zl

    def dev(x, y, z, c):
        return {"section": x * 2 + z // NZL, "dp": (y * NZL + z % NZL) * 2 + c}

    mate = dev(x, y, z, 1 - c)

    places = (x * 2 + c, y, z)
    members = (
        lambda m: dev(m // 2, y, z, m % 2),
        lambda m: dev(x, m, z, c),
        lambda m: dev(x, y, m, c),
    )
    place_a = zl * 2 + c
    member_a = lambda m: dev(x, y, zh * NZL + m // 2, m % 2)

    barrier = pltpu.get_barrier_semaphore()

    def greet(members, place):
        def one(r, _):
            pl.semaphore_signal(
                barrier, inc=1, device_id=members((place + r) % 8), device_id_type=MESH
            )
            return 0

        lax.fori_loop(1, 8, one, 0)

    loads = [
        pltpu.make_async_copy(og_hbm, og, load_sem.at[0]),
        pltpu.make_async_copy(acts_hbm, acts, load_sem.at[1]),
        pltpu.make_async_copy(master_hbm, state.at[0], load_sem.at[2]),
        pltpu.make_async_copy(one_hbm, state.at[1], load_sem.at[3]),
        pltpu.make_async_copy(two_hbm, state.at[2], load_sem.at[4]),
    ]
    for load in loads:
        load.start()
    for p in range(3):
        greet(members[p], places[p])
    greet(member_a, place_a)

    loads[1].wait()
    loads[0].wait()
    grad = lax.dot_general(
        acts[...], og[...], (((1,), (1,)), ((), ())), preferred_element_type=jnp.float32
    )
    state[3] = grad
    norms[0, places[0]] = jnp.broadcast_to(jnp.sum(grad * grad), (1, 128))
    pl.semaphore_wait(barrier, 28)

    def norm_start(p):
        def one(r, _):
            pltpu.make_async_remote_copy(
                src_ref=norms.at[p, places[p]],
                dst_ref=norms.at[p, places[p]],
                send_sem=norm_send.at[p],
                recv_sem=norm_recv.at[p],
                device_id=members[p]((places[p] + r) % 8),
                device_id_type=MESH,
            ).start()
            return 0

        lax.fori_loop(1, 8, one, 0)

    def drain(ref, sem):
        pltpu.make_async_copy(ref, ref, sem).wait()

    def norm_finish(p):
        drain(norms.at[p, pl.ds(0, 7)], norm_recv.at[p])
        return jnp.sum(norms[p], axis=0)

    norm_start(0)

    for load in loads[2:]:
        load.wait()
    theirs = pl.ds(pl.multiple_of((1 - c) * HALF, HALF), HALF)
    mine = pl.ds(pl.multiple_of(c * HALF, HALF), HALF)
    for i in range(4):
        pltpu.make_async_remote_copy(
            src_ref=state.at[i, theirs],
            dst_ref=other.at[i],
            send_sem=pair_send.at[i],
            recv_sem=pair_recv.at[i],
            device_id=mate,
            device_id_type=MESH,
        ).start()

    weights = state[0].astype(jnp.bfloat16)
    partial = jnp.dot(weights, og[...], preferred_element_type=jnp.float32)
    turned = partial.T
    for j in range(8):
        for q in range(2):
            rows = [(4 * q + i) * 64 + j * 8 for i in range(4)]
            parts_a[j, q] = jnp.concatenate([turned[r : r + 8] for r in rows], axis=1)
    got_a[place_a] = parts_a[place_a]

    total = norm_finish(0)
    norms[1, places[1]] = total
    norm_start(1)

    def a_start(r, _):
        m = (place_a + r) % 8
        pltpu.make_async_remote_copy(
            src_ref=parts_a.at[m],
            dst_ref=got_a.at[place_a],
            send_sem=a_send,
            recv_sem=a_recv,
            device_id=member_a(m),
            device_id_type=MESH,
        ).start()
        return 0

    lax.fori_loop(1, 8, a_start, 0)

    total = norm_finish(1)
    norms[2, places[2]] = total
    norm_start(2)

    drain(got_a.at[pl.ds(0, 7)], a_recv)
    part_b[...] = jnp.sum(got_a[...], axis=0)
    for i in range(4):
        drain(other.at[i], pair_recv.at[i])

    total = norm_finish(2)
    limit = math.sqrt(8 * FF * SLAB)
    clip = jnp.minimum(1.0, limit / jnp.sqrt(total + 1e-06))[:, :1]

    own_w, _, _ = adam(state[0, mine], state[3, mine], state[1, mine], state[2, mine], clip)
    mate_w, _, _ = adam(other[0], other[3], other[1], other[2], clip)
    first = jnp.where(c == 0, own_w, mate_w)
    second = jnp.where(c == 0, mate_w, own_w)
    block = y * NZL + zl
    w_out[block, c] = jnp.concatenate([first, second], axis=1).astype(jnp.bfloat16)

    step = 1 - 2 * c
    ring_to = dev(x, (y + step + NY) % NY, z, c)

    def full(b):
        return w_out.at[b, c]

    def low(b):
        return w_out.at[b, c, :, pl.ds(0, CUT)]

    def high(b):
        return w_out.at[b, c, :, pl.ds(CUT, WIDE - CUT)]

    def send(ref, to, send_sem, recv_sem):
        pltpu.make_async_remote_copy(
            src_ref=ref, dst_ref=ref, send_sem=send_sem, recv_sem=recv_sem,
            device_id=to, device_id_type=MESH,
        ).start()

    def z_other(j):
        return (zl + j) % NZL

    def z_dev(j):
        return dev(x, y, zh * NZL + z_other(j), c)

    send(full(block), ring_to, ring_full_send, ring_recv.at[block])
    for j in (1, 3, 2):
        send(full(block), z_dev(j), z_full_send, z_full_recv.at[zl])
    send(full(block), mate, core_send, core_recv)

    new_master, new_one, new_two = adam(state[0], state[3], state[1], state[2], clip)
    master_out[...] = new_master
    one_out[...] = new_one
    two_out[...] = new_two

    @pl.when(s > 0)
    def _():
        def b_start(m, _):
            pltpu.make_async_remote_copy(
                src_ref=part_b.at[m // 4],
                dst_ref=got_b.at[y],
                send_sem=b_send,
                recv_sem=b_recv,
                device_id={"section": s - 1, "dp": (m * NZL + zl) * 2 + c},
                device_id_type=MESH,
            ).start()
            return 0

        lax.fori_loop(0, NY, b_start, 0)

    def source(k):
        return ((y - step * k + 2 * NY) % NY) * NZL

    def z_home(j):
        b = y * NZL + z_other(j)
        drain(full(b), z_full_recv.at[z_other(j)])
        send(low(b), ring_to, ring_cut_send, ring_recv.at[b])
        send(full(b), mate, core_send, core_recv)

    def ring_own(k, cut_now, last):
        b = source(k) + zl
        drain(full(b), ring_recv.at[b])
        if not last:
            send(full(b), ring_to, ring_full_send, ring_recv.at[b])
        if cut_now:
            for j in (1, 3, 2):
                send(high(b), z_dev(j), z_cut_send, z_cut_recv.at[b])
        send(full(b), mate, core_send, core_recv)

    def ring_other(k, j, cut_now, cut_next, last):
        b = source(k) + z_other(j)
        ref = low(b) if cut_now else full(b)
        drain(ref, ring_recv.at[b])
        if not last:
            if cut_next:
                send(low(b), ring_to, ring_cut_send, ring_recv.at[b])
            else:
                send(full(b), ring_to, ring_full_send, ring_recv.at[b])
        send(ref, mate, core_send, core_recv)

    def z_high(k):
        for j in (1, 3, 2):
            b = source(k) + z_other(j)
            drain(high(b), z_cut_recv.at[b])
            send(high(b), mate, core_send, core_recv)

    ring_own(1, True, False)
    for j in (1, 3, 2):
        z_home(j)
    for k in range(1, NY):
        if k > 1:
            ring_own(k, k <= SPLIT_STEPS, k == NY - 1)
        if k == SPLIT_STEPS:
            z_high(k - 2)
            z_high(k - 1)
            z_high(k)
        elif 3 <= k < SPLIT_STEPS:
            z_high(k - 2)
        for j in (1, 3, 2):
            ring_other(k, j, k <= SPLIT_STEPS, k + 1 <= SPLIT_STEPS, k == NY - 1)

    @pl.when(s < 7)
    def _():
        drain(got_b, b_recv)
        tile = jnp.sum(got_b[...], axis=0)
        tile = pltpu.roll(tile, (128 - (y % 4) * SLAB) % 128, 1)
        prev_out[...] = tile[:, :SLAB].astype(jnp.bfloat16)

    @pl.when(s == 7)
    def _():
        prev_out[...] = jnp.zeros_like(prev_out)

    for p in range(3):
        drain(norms.at[p, pl.ds(0, 7)], norm_send.at[p])
    for i in range(4):
        drain(other.at[i], pair_send.at[i])
    drain(got_a.at[pl.ds(0, 7)], a_send)

    @pl.when(s > 0)
    def _():
        drain(got_b, b_send)

    n_cut = 3 * SPLIT_STEPS
    n_full = 4 * (NY - 1) - n_cut
    drain(w_out.at[pl.ds(0, n_full), c], ring_full_send)
    drain(w_out.at[pl.ds(0, n_cut), c, :, pl.ds(0, CUT)], ring_cut_send)
    drain(w_out.at[pl.ds(0, 3), c], z_full_send)
    drain(w_out.at[pl.ds(0, n_cut), c, :, pl.ds(CUT, WIDE - CUT)], z_cut_send)
    drain(w_out.at[:, 1 - c], core_recv)
    drain(w_out.at[:, c], core_send)


def write_kernel(
    w, master, one, two, prev, prev_hbm, master_hbm, one_hbm, two_hbm, w_hbm, sem
):
    copies = []
    for b in range(32):
        for h in range(2):
            copies.append(
                pltpu.make_async_copy(
                    w.at[b, h],
                    w_hbm.at[0, pl.ds(h * HALF, HALF), pl.ds(b * WIDE, WIDE)],
                    sem.at[b],
                )
            )
    small = [
        pltpu.make_async_copy(prev, prev_hbm.at[0], sem.at[32]),
        pltpu.make_async_copy(master, master_hbm.at[0], sem.at[33]),
        pltpu.make_async_copy(one, one_hbm.at[0], sem.at[34]),
        pltpu.make_async_copy(two, two_hbm.at[0], sem.at[35]),
    ]
    for copy in small + copies:
        copy.start()
    for copy in small + copies:
        copy.wait()


def body(activations, out_grads, master, moment_one, moment_two):
    f32, bf16 = jnp.float32, jnp.bfloat16
    hbm = pl.BlockSpec(memory_space=pltpu.HBM)
    vmem = pl.BlockSpec(memory_space=pltpu.VMEM)
    dma = pltpu.SemaphoreType.DMA
    kept = pl.pallas_call(
        main_kernel,
        out_shape=(
            pltpu.VMEM((32, 2, HALF, WIDE), bf16),
            pltpu.VMEM((SLAB, COLS), f32),
            pltpu.VMEM((SLAB, COLS), f32),
            pltpu.VMEM((SLAB, COLS), f32),
            pltpu.VMEM((8, SLAB), bf16),
        ),
        in_specs=[hbm] * 5,
        out_specs=[vmem] * 5,
        scratch_shapes=[
            pltpu.VMEM((SLAB, 512), bf16),
            pltpu.VMEM((COLS, 512), bf16),
            pltpu.VMEM((4, SLAB, COLS), f32),
            pltpu.VMEM((4, HALF, COLS), f32),
            pltpu.VMEM((3, 8, 1, 128), f32),
            pltpu.VMEM((8, 2, 8, 128), f32),
            pltpu.VMEM((8, 2, 8, 128), f32),
            pltpu.VMEM((2, 8, 128), f32),
            pltpu.VMEM((8, 8, 128), f32),
            dma((5,)), dma((3,)), dma((3,)), dma((4,)), dma((4,)),
            dma, dma, dma, dma,
            dma, dma, dma((32,)),
            dma, dma, dma, dma, dma((4,)), dma((32,)),
        ],
        compiler_params=pltpu.CompilerParams(
            collective_id=0, has_side_effects=True, vmem_limit_bytes=VMEM_GRANT
        ),
        name="update_and_gather",
    )(
        activations[0],
        jnp.swapaxes(out_grads, 1, 2)[0],
        master[0],
        moment_one[0],
        moment_two[0],
    )
    shapes = (
        jax.ShapeDtypeStruct((1, 8, SLAB), bf16),
        jax.ShapeDtypeStruct((1, SLAB, COLS), f32),
        jax.ShapeDtypeStruct((1, SLAB, COLS), f32),
        jax.ShapeDtypeStruct((1, SLAB, COLS), f32),
        jax.ShapeDtypeStruct((1, SLAB, FF), bf16),
    )
    return pl.pallas_call(
        write_kernel,
        out_shape=shapes,
        in_specs=[vmem] * 5,
        out_specs=[hbm] * 5,
        scratch_shapes=[dma((36,))],
        compiler_params=pltpu.CompilerParams(vmem_limit_bytes=8 << 20),
        name="write_out",
    )(*kept)


def solution(mesh):
    placed = (
        P("section", None, None),
        P("section", None, "dp"),
        P("section", None, "dp"),
        P("section", None, "dp"),
        P("section", None, "dp"),
    )
    return jax.shard_map(
        body,
        mesh=mesh,
        in_specs=placed,
        out_specs=(
            P("section", "dp", None),
            P("section", None, "dp"),
            P("section", None, "dp"),
            P("section", None, "dp"),
            P("section", None, None),
        ),
        check_vma=False,
    )
```

time: 457 us -> 63.5 us (0.14); the launches traced: 450 us -> 63.3 us
  blocking collectives: 370 us -> 0 us
  Pallas kernels: 0 us -> 62.7 us
  local copies, waits for them, and re-layouts: 52.7 us -> 0 us
  between operations: 14.8 us -> 0.64 us
  waiting for transfers between devices: 6.95 us -> 0 us
    psum x2 -> x0, blocking collectives: 370 us -> none  [the longest x1 264 us: body(): lax.psum(lax.dot_general(grads_local, weights[0], (((1,), (1,)), ((), ())...]
    pallas_call x0 -> x2, Pallas kernels: none -> 62.7 us  [the longest x1 60.5 us: body(): pl.pallas_call(main_kernel, out_shape=(pltpu.VMEM((32, 2, HALF, WIDE), bf...]
    unnamed x4 -> x0, local copies, waits for them, and re-layouts: 51.7 us -> none
    ppermute x1 -> x0, waiting for transfers between devices: 6.94 us -> none  [shifted(): return lax.ppermute(value, axis, pairs)]
  transfers between devices with their start and end apart: 2 -> 0, of which waited for: 1 -> 0; matrix products, arithmetic and copies ran while one was open for 0% -> 0% of each run, Pallas kernels for 0% -> 0%
where the time goes in v1:
time: 63.5 us; the launch traced here: 63.3 us
  Pallas kernels  62.7 us (99%)
  between operations  0.64 us (1%)
    pallas_call x1, Pallas kernels, body(): pl.pallas_call(main_kernel, out_shape=(pltpu.VMEM((32, 2, HALF, WIDE), bf...  60.5 us
    pallas_call x1, Pallas kernels, body(): pl.pallas_call(write_kernel, out_shape=shapes, in_specs=[vmem] * 5, out_s...  2.16 us

profile of v1, /device:TPU:1, one launch (start us, length us, event | category | flops | bytes accessed | tf_op | source)
XLA Modules:
  0.0 63.3 jit_solution(12526683491781235729)
XLA Ops:
  0.6 60.5 %update_and_gather.1 = (bf16[32,2,16,1664]{3,2,1,0:T(8,128)(2,1)S(1)}, f32[32,832]{1,0:T(8,128)S(1)}, f32[32,832]{1,0:T(8,128)S(1)}, f32[32,832]{1,0:T(8,128)S(1)}, bf16[8,32]{1,0:T(8,128)(2,1)S(1)}) custom-call(bf16[32,512]{1,0:T(8,128)(2,1)} %bitcast.11, bf16[832,512]{1,0:T(8,128)(2,1)} %bitcast.7, f32[32,832]{1,0:T(8,128)} %bitcast.8, f32[32,832]{1,0:T(8,128)} %bitcast.9, ...), custom_call_target="tpu_custom_call" | custom-call | tf_op jit(solution)/shard_map/update_and_gather/pallas_call | solution.py:341
  61.2 2.2 %write_out.1 = (bf16[1,8,32]{2,1,0:T(8,128)(2,1)}, f32[1,32,832]{2,1,0:T(8,128)}, f32[1,32,832]{2,1,0:T(8,128)}, f32[1,32,832]{2,1,0:T(8,128)}, bf16[1,32,53248]{2,1,0:T(8,128)(2,1)}) custom-call(bf16[32,2,16,1664]{3,2,1,0:T(8,128)(2,1)S(1)} %get-tuple-element.10.w, f32[32,832]{1,0:T(8,128)S(1)} %get-tuple-element.11.master, ...), custom_call_target="tpu_custom_call" | custom-call | tf_op jit(solution)/shard_map/write_out/pallas_call | solution.py:385

commit v2 on v1

v2 whole, which is shorter than its diff:
```python
import functools
import math

import jax
import jax.numpy as jnp
from jax import lax
from jax.experimental import pallas as pl
from jax.experimental.pallas import tpu as pltpu
from jax.sharding import PartitionSpec as P

FF = 53248
SLAB = 32
MESH = pl.DeviceIdType.MESH

NX, NY, NZ, NZL = 4, 8, 8, 4
COLS = FF // 64
WIDE = 2 * COLS
HALF = SLAB // 2
def hops(by, size):
    return min(by, size - by)


NEAR_STEPS = sorted(
    ((dz, dc) for dz in range(NZ) for dc in range(2) if dz or dc), key=lambda m: -hops(m[0], NZ)
)
FLAT_STEPS = sorted(
    ((dx, dy) for dx in range(NX) for dy in range(NY) if dx or dy),
    key=lambda m: -hops(m[0], NX) - hops(m[1], NY),
)
REACH = {1: 4, -1: 3}
OWN_HOPS = ((3, 4), (2, 3), (1, 2), (0, 1))
OTHER_HOPS = ((2, 4), (2, 3), (1, 2), (0, 1))
CUTS = (11, 11, 9, 9, 9)
TILES = WIDE // 128
ORDER = (
    ("own", 1, 1, 0), ("own", -1, 1, 0), ("home", 1, 0, 3), ("home", 1, 0, 1), ("high", 1, 0, 3),
    ("high", 1, 0, 1), ("own", 1, 2, 0), ("high", 1, 1, 3), ("own", -1, 2, 0), ("home", 1, 0, 2),
    ("high", 1, 1, 1), ("high", 1, 0, 2), ("high", -1, 1, 3), ("high", -1, 1, 1), ("high", 1, 1, 2),
    ("low", 1, 1, 3), ("low", -1, 1, 3), ("high", -1, 1, 2), ("low", 1, 1, 1), ("low", -1, 1, 1),
    ("high", 1, 2, 3), ("high", 1, 2, 1), ("own", 1, 3, 0), ("high", -1, 2, 3), ("low", 1, 1, 2),
    ("high", 1, 2, 2), ("high", -1, 2, 1), ("low", -1, 1, 2), ("own", -1, 3, 0), ("low", 1, 2, 3),
    ("high", -1, 2, 2), ("low", -1, 2, 3), ("low", 1, 2, 1), ("low", -1, 2, 1), ("low", 1, 2, 2),
    ("low", -1, 2, 2), ("high", 1, 3, 3), ("high", 1, 3, 1), ("own", 1, 4, 0), ("high", 1, 3, 2),
    ("high", -1, 3, 3), ("low", -1, 3, 3), ("high", -1, 3, 1), ("high", -1, 3, 2), ("low", 1, 3, 3),
    ("low", -1, 3, 1), ("low", 1, 4, 3), ("low", -1, 3, 2), ("low", 1, 3, 1), ("low", 1, 4, 1),
    ("low", 1, 3, 2), ("low", 1, 4, 2), ("high", 1, 4, 3), ("high", 1, 4, 1), ("high", 1, 4, 2),
)
VMEM_GRANT = 63250000


def adam(master, grad, one, two, clip):
    scaled = clip * grad
    new_one = 0.9 * one + 0.1 * scaled
    new_two = 0.95 * two + 0.05 * scaled * scaled
    new_master = master - 0.05 * (new_one / (1.0 - 0.9**10)) / (
        jnp.sqrt(new_two / (1.0 - 0.95**10)) + 1e-08
    )
    return new_master, new_one, new_two


def main_kernel(
    acts_hbm, og_hbm, master_hbm, one_hbm, two_hbm,
    w_out, master_out, one_out, two_out, prev_out,
    acts, og, state, other, norms_near, norms_flat, turned, parts_a, got_a, part_b, got_b,
    load_sem, norm_send, norm_recv, pair_send, pair_recv,
    a_send, a_recv, b_send, b_recv,
    gather_send, ring_recv, core_send, core_recv, z_full_recv, z_cut_recv,
):
    s = lax.axis_index("section")
    d = lax.axis_index("dp")
    div, rem = lax.div, lax.rem
    norms = (norms_near, norms_flat)
    x, zh = div(s, 2), rem(s, 2)
    y, zl, c = div(d, 8), rem(div(d, 2), NZL), rem(d, 2)
    z = zh * NZL + zl

    def dev(x, y, z, c):
        return {"section": x * 2 + div(z, NZL), "dp": (y * NZL + rem(z, NZL)) * 2 + c}

    mate = dev(x, y, z, 1 - c)

    def ring8(a, by):
        return rem(a + by, 8)

    near = [dev(x, y, ring8(z, dz), rem(c + dc, 2)) for dz, dc in NEAR_STEPS]
    flat = [dev(rem(x + dx, NX), ring8(y, dy), z, c) for dx, dy in FLAT_STEPS]
    groups = (near, flat)
    places = (z * 2 + c, x * NY + y)
    place_a = zl * 2 + c
    group_a = [
        (rem(zl + dz, NZL) * 2 + rem(c + dc, 2), rem(zl + dz, NZL), rem(c + dc, 2))
        for dz in range(NZL)
        for dc in range(2)
        if dz or dc
    ]

    barrier = pltpu.get_barrier_semaphore()

    def greet(who):
        pl.semaphore_signal(barrier, inc=1, device_id=who, device_id_type=MESH)

    loads = [
        pltpu.make_async_copy(og_hbm, og, load_sem.at[0]),
        pltpu.make_async_copy(acts_hbm, acts, load_sem.at[1]),
        pltpu.make_async_copy(master_hbm, state.at[0], load_sem.at[2]),
        pltpu.make_async_copy(one_hbm, state.at[1], load_sem.at[3]),
        pltpu.make_async_copy(two_hbm, state.at[2], load_sem.at[4]),
    ]
    for load in loads:
        load.start()
    for group in groups:
        for who in group:
            greet(who)

    loads[1].wait()
    loads[0].wait()
    grad = lax.dot_general(
        acts[...], og[...], (((1,), (1,)), ((), ())), preferred_element_type=jnp.float32
    )
    state[3] = grad
    norms[0][places[0]] = jnp.broadcast_to(jnp.sum(grad * grad), (1, 128))
    pl.semaphore_wait(barrier, len(groups[0]) + len(groups[1]))

    def norm_start(p):
        for who in groups[p]:
            pltpu.make_async_remote_copy(
                src_ref=norms[p].at[places[p]],
                dst_ref=norms[p].at[places[p]],
                send_sem=norm_send.at[p],
                recv_sem=norm_recv.at[p],
                device_id=who,
                device_id_type=MESH,
            ).start()

    def drain(ref, sem):
        pltpu.make_async_copy(ref, ref, sem).wait()

    def norm_finish(p):
        drain(norms[p].at[pl.ds(0, len(groups[p]))], norm_recv.at[p])
        return jnp.sum(norms[p][...], axis=0)

    norm_start(0)

    for load in loads[2:]:
        load.wait()
    theirs = pl.ds(pl.multiple_of((1 - c) * HALF, HALF), HALF)
    mine = pl.ds(pl.multiple_of(c * HALF, HALF), HALF)
    for i in range(4):
        pltpu.make_async_remote_copy(
            src_ref=state.at[i, theirs],
            dst_ref=other.at[i],
            send_sem=pair_send.at[i],
            recv_sem=pair_recv.at[i],
            device_id=mate,
            device_id_type=MESH,
        ).start()

    weights = state[0].astype(jnp.bfloat16)
    partial = jnp.dot(weights, og[...], preferred_element_type=jnp.float32)
    turned[...] = partial.T
    for j in range(8):
        for u in range(2):
            rows = [pl.ds(j * 8 + u * 4 + i, NY, stride=64) for i in range(4)]
            parts_a[j, u] = jnp.concatenate([turned[r] for r in rows], axis=1)
    got_a[place_a] = parts_a[place_a]
    for m, to_zl, to_c in group_a:
        pltpu.make_async_remote_copy(
            src_ref=parts_a.at[m],
            dst_ref=got_a.at[place_a],
            send_sem=a_send,
            recv_sem=a_recv,
            device_id=dev(x, y, zh * NZL + to_zl, to_c),
            device_id_type=MESH,
        ).start()

    total = norm_finish(0)
    norms[1][places[1]] = total
    norm_start(1)

    drain(got_a.at[pl.ds(0, 7)], a_recv)
    for u in range(2):
        rows = jnp.sum(got_a[:, u], axis=0)
        for m in range(NY):
            part_b[m, u] = rows[m]

    for i in range(4):
        drain(other.at[i], pair_recv.at[i])

    total = norm_finish(1)
    limit = math.sqrt(8 * FF * SLAB)
    clip = jnp.minimum(1.0, limit / jnp.sqrt(total + 1e-06))[:, :1]

    own_w, _, _ = adam(state[0, mine], state[3, mine], state[1, mine], state[2, mine], clip)
    mate_w, _, _ = adam(other[0], other[3], other[1], other[2], clip)
    first = jnp.where(c == 0, own_w, mate_w)
    second = jnp.where(c == 0, mate_w, own_w)
    block = y * NZL + zl
    whole = jnp.concatenate([first, second], axis=1).astype(jnp.bfloat16)
    w_out[c, block] = whole

    ahead = 1 - 2 * c

    def ring_to(side, hops):
        return dev(x, rem(y + ahead * side * hops + NY, NY), z, c)

    def tiles(b, start, stop):
        return w_out.at[c, b, :, pl.ds(start * 128, (stop - start) * 128)]

    sent = {}

    def send(b, start, stop, to, recv_sem):
        size = stop - start
        sent[size] = sent.get(size, 0) + 1
        ref = tiles(b, start, stop)
        pltpu.make_async_remote_copy(
            src_ref=ref, dst_ref=ref, send_sem=gather_send.at[size], recv_sem=recv_sem,
            device_id=to, device_id_type=MESH,
        ).start()

    def to_mate(b, start, stop):
        ref = tiles(b, start, stop)
        pltpu.make_async_remote_copy(
            src_ref=ref, dst_ref=ref, send_sem=core_send, recv_sem=core_recv,
            device_id=mate, device_id_type=MESH,
        ).start()

    def z_other(j):
        return rem(zl + j, NZL)

    def z_dev(j):
        return dev(x, y, zh * NZL + z_other(j), c)

    def own_on(b, side, k):
        for start, stop in OWN_HOPS:
            if start == k and stop <= REACH[side]:
                send(b, 0, TILES, ring_to(side, stop - start), ring_recv.at[b])

    def other_on(b, side, k):
        for start, stop in OTHER_HOPS:
            if start == k and stop <= REACH[side] and CUTS[stop]:
                send(b, 0, CUTS[stop], ring_to(side, stop - start), ring_recv.at[b])

    def high_on(b, k):
        if CUTS[k] < TILES:
            for j in (1, 3, 2):
                send(b, CUTS[k], TILES, z_dev(j), z_cut_recv.at[b])

    for side in REACH:
        own_on(block, side, 0)
    for j in (1, 3, 2):
        send(block, 0, CUTS[0], z_dev(j), z_full_recv.at[zl])
    high_on(block, 0)
    to_mate(block, 0, TILES)

    @pl.when(s > 0)
    def _():
        for m in range(NY):
            pltpu.make_async_remote_copy(
                src_ref=part_b.at[m],
                dst_ref=got_b.at[y],
                send_sem=b_send,
                recv_sem=b_recv,
                device_id={"section": s - 1, "dp": (m * NZL + zl) * 2 + c},
                device_id_type=MESH,
            ).start()

    new_master, new_one, new_two = adam(state[0], state[3], state[1], state[2], clip)
    master_out[...] = new_master
    one_out[...] = new_one
    two_out[...] = new_two

    def source(side, k):
        return rem(y - ahead * side * k + NY, NY) * NZL

    for what, side, k, j in ORDER:
        b = source(side, k) + z_other(j)
        if what == "own":
            drain(tiles(b, 0, TILES), ring_recv.at[b])
            own_on(b, side, k)
            high_on(b, k)
            to_mate(b, 0, TILES)
        elif what == "home":
            drain(tiles(b, 0, CUTS[0]), z_full_recv.at[z_other(j)])
            for out in REACH:
                other_on(b, out, 0)
            to_mate(b, 0, CUTS[0])
        elif what == "low":
            drain(tiles(b, 0, CUTS[k]), ring_recv.at[b])
            other_on(b, side, k)
            to_mate(b, 0, CUTS[k])
        else:
            drain(tiles(b, CUTS[k], TILES), z_cut_recv.at[b])
            to_mate(b, CUTS[k], TILES)

    @pl.when(s < 7)
    def _():
        drain(got_b, b_recv)
        rows = jnp.sum(got_b[...], axis=0)
        rows = [rows[u : u + 1, i * SLAB : (i + 1) * SLAB] for u in range(2) for i in range(4)]
        prev_out[...] = jnp.concatenate(rows, axis=0).astype(jnp.bfloat16)

    @pl.when(s == 7)
    def _():
        prev_out[...] = jnp.zeros_like(prev_out)

    for p, group in enumerate(groups):
        drain(norms[p].at[pl.ds(0, len(group))], norm_send.at[p])
    for i in range(4):
        drain(other.at[i], pair_send.at[i])
    drain(got_a.at[pl.ds(0, 7)], a_send)

    @pl.when(s > 0)
    def _():
        drain(got_b, b_send)

    for size, count in sorted(sent.items()):
        drain(w_out.at[0, pl.ds(0, count), :, pl.ds(0, size * 128)], gather_send.at[size])
    drain(w_out.at[1 - c], core_recv)
    drain(w_out.at[c], core_send)


def write_kernel(
    w, master, one, two, prev, prev_hbm, master_hbm, one_hbm, two_hbm, w_hbm, sem
):
    copies = []
    for h in range(2):
        rows = pl.ds(h * HALF, HALF)
        for b in range(32):
            copies.append(
                pltpu.make_async_copy(w.at[h, b], w_hbm.at[0, rows, pl.ds(b * WIDE, WIDE)], sem.at[b])
            )
    small = [
        pltpu.make_async_copy(prev, prev_hbm.at[0], sem.at[32 + 0]),
        pltpu.make_async_copy(master, master_hbm.at[0], sem.at[32 + 1]),
        pltpu.make_async_copy(one, one_hbm.at[0], sem.at[32 + 2]),
        pltpu.make_async_copy(two, two_hbm.at[0], sem.at[32 + 3]),
    ]
    for copy in small + copies:
        copy.start()
    for copy in small + copies:
        copy.wait()


def body(activations, out_grads, master, moment_one, moment_two):
    f32, bf16 = jnp.float32, jnp.bfloat16
    hbm = pl.BlockSpec(memory_space=pltpu.HBM)
    vmem = pl.BlockSpec(memory_space=pltpu.VMEM)
    dma = pltpu.SemaphoreType.DMA
    kept = pl.pallas_call(
        main_kernel,
        out_shape=(
            pltpu.VMEM((2, 32, HALF, WIDE), bf16),
            pltpu.VMEM((SLAB, COLS), f32),
            pltpu.VMEM((SLAB, COLS), f32),
            pltpu.VMEM((SLAB, COLS), f32),
            pltpu.VMEM((8, SLAB), bf16),
        ),
        in_specs=[hbm] * 5,
        out_specs=[vmem] * 5,
        scratch_shapes=[
            pltpu.VMEM((SLAB, 512), bf16),
            pltpu.VMEM((COLS, 512), bf16),
            pltpu.VMEM((4, SLAB, COLS), f32),
            pltpu.VMEM((4, HALF, COLS), f32),
            pltpu.VMEM((2 * NZ, 1, 128), f32),
            pltpu.VMEM((NX * NY, 1, 128), f32),
            pltpu.VMEM((512, SLAB), f32),
            pltpu.VMEM((8, 2, NY, 128), f32),
            pltpu.VMEM((8, 2, NY, 128), f32),
            pltpu.VMEM((NY, 2, 128), f32),
            pltpu.VMEM((NY, 2, 128), f32),
            dma((5,)), dma((2,)), dma((2,)), dma((4,)), dma((4,)),
            dma, dma, dma, dma,
            dma((TILES + 1,)), dma((32,)), dma, dma, dma((NZL,)), dma((32,)),
        ],
        compiler_params=pltpu.CompilerParams(
            collective_id=0, has_side_effects=True, vmem_limit_bytes=VMEM_GRANT
        ),
        name="update_and_gather",
    )(
        activations[0],
        jnp.swapaxes(out_grads, 1, 2)[0],
        master[0],
        moment_one[0],
        moment_two[0],
    )
    shapes = (
        jax.ShapeDtypeStruct((1, 8, SLAB), bf16),
        jax.ShapeDtypeStruct((1, SLAB, COLS), f32),
        jax.ShapeDtypeStruct((1, SLAB, COLS), f32),
        jax.ShapeDtypeStruct((1, SLAB, COLS), f32),
        jax.ShapeDtypeStruct((1, SLAB, FF), bf16),
    )
    return pl.pallas_call(
        write_kernel,
        out_shape=shapes,
        in_specs=[vmem] * 5,
        out_specs=[hbm] * 5,
        scratch_shapes=[dma((36,))],
        compiler_params=pltpu.CompilerParams(vmem_limit_bytes=8 << 20),
        name="write_out",
    )(*kept)


def solution(mesh):
    placed = (
        P("section", None, None),
        P("section", None, "dp"),
        P("section", None, "dp"),
        P("section", None, "dp"),
        P("section", None, "dp"),
    )
    return jax.shard_map(
        body,
        mesh=mesh,
        in_specs=placed,
        out_specs=(
            P("section", "dp", None),
            P("section", None, "dp"),
            P("section", None, "dp"),
            P("section", None, "dp"),
            P("section", None, None),
        ),
        check_vma=False,
    )
```

time: 63.5 us -> 52.2 us (0.82)
  Pallas kernels: 62.7 us -> 51.4 us
    pallas_call x1, Pallas kernels: 60.5 us -> 49.2 us  [body(): pl.pallas_call(main_kernel, out_shape=(pltpu.VMEM((2, 32, HALF, WIDE), bf...]
where the time goes in v2:
time: 52.2 us; the launch traced here: 52 us
  Pallas kernels  51.4 us (98%)
  between operations  0.64 us (1%)
    pallas_call x1, Pallas kernels, body(): pl.pallas_call(main_kernel, out_shape=(pltpu.VMEM((2, 32, HALF, WIDE), bf...  49.2 us
    pallas_call x1, Pallas kernels, body(): pl.pallas_call(write_kernel, out_shape=shapes, in_specs=[vmem] * 5, out_s...  2.16 us

profile of v2, /device:TPU:1, one launch (start us, length us, event | category | flops | bytes accessed | tf_op | source)
XLA Modules:
  0.0 52.0 jit_solution(10051190469586901154)
XLA Ops:
  0.6 49.2 %update_and_gather.1 = (bf16[2,32,16,1664]{3,2,1,0:T(8,128)(2,1)S(1)}, f32[32,832]{1,0:T(8,128)S(1)}, f32[32,832]{1,0:T(8,128)S(1)}, f32[32,832]{1,0:T(8,128)S(1)}, bf16[8,32]{1,0:T(8,128)(2,1)S(1)}) custom-call(bf16[32,512]{1,0:T(8,128)(2,1)} %bitcast.11, bf16[832,512]{1,0:T(8,128)(2,1)} %bitcast.7, f32[32,832]{1,0:T(8,128)} %bitcast.8, f32[32,832]{1,0:T(8,128)} %bitcast.9, ...), custom_call_target="tpu_custom_call" | custom-call | tf_op jit(solution)/shard_map/update_and_gather/pallas_call | solution.py:349
  49.9 2.2 %write_out.1 = (bf16[1,8,32]{2,1,0:T(8,128)(2,1)}, f32[1,32,832]{2,1,0:T(8,128)}, f32[1,32,832]{2,1,0:T(8,128)}, f32[1,32,832]{2,1,0:T(8,128)}, bf16[1,32,53248]{2,1,0:T(8,128)(2,1)}) custom-call(bf16[2,32,16,1664]{3,2,1,0:T(8,128)(2,1)S(1)} %get-tuple-element.10.w, f32[32,832]{1,0:T(8,128)S(1)} %get-tuple-element.11.master, ...), custom_call_target="tpu_custom_call" | custom-call | tf_op jit(solution)/shard_map/write_out/pallas_call | solution.py:394

commit v3 on v2

--- a/solution.py
+++ b/solution.py
@@ -30,20 +30,21 @@
 REACH = {1: 4, -1: 3}
 OWN_HOPS = ((3, 4), (2, 3), (1, 2), (0, 1))
 OTHER_HOPS = ((2, 4), (2, 3), (1, 2), (0, 1))
-CUTS = (11, 11, 9, 9, 9)
+CUTS = (10, 10, 9, 9, 9)
 TILES = WIDE // 128
+HAND_OFF_TURN = 14
 ORDER = (
     ("own", 1, 1, 0), ("own", -1, 1, 0), ("home", 1, 0, 3), ("home", 1, 0, 1), ("high", 1, 0, 3),
-    ("high", 1, 0, 1), ("own", 1, 2, 0), ("high", 1, 1, 3), ("own", -1, 2, 0), ("home", 1, 0, 2),
-    ("high", 1, 1, 1), ("high", 1, 0, 2), ("high", -1, 1, 3), ("high", -1, 1, 1), ("high", 1, 1, 2),
-    ("low", 1, 1, 3), ("low", -1, 1, 3), ("high", -1, 1, 2), ("low", 1, 1, 1), ("low", -1, 1, 1),
-    ("high", 1, 2, 3), ("high", 1, 2, 1), ("own", 1, 3, 0), ("high", -1, 2, 3), ("low", 1, 1, 2),
-    ("high", 1, 2, 2), ("high", -1, 2, 1), ("low", -1, 1, 2), ("own", -1, 3, 0), ("low", 1, 2, 3),
+    ("high", 1, 0, 1), ("own", 1, 2, 0), ("home", 1, 0, 2), ("own", -1, 2, 0), ("high", 1, 1, 3),
+    ("high", 1, 1, 1), ("high", 1, 0, 2), ("high", -1, 1, 3), ("low", 1, 1, 3), ("high", -1, 1, 1),
+    ("low", -1, 1, 3), ("high", 1, 1, 2), ("low", 1, 1, 1), ("low", -1, 1, 1), ("high", -1, 1, 2),
+    ("high", 1, 2, 3), ("high", 1, 2, 1), ("own", 1, 3, 0), ("low", -1, 1, 2), ("low", 1, 1, 2),
+    ("high", -1, 2, 3), ("high", 1, 2, 2), ("high", -1, 2, 1), ("own", -1, 3, 0), ("low", 1, 2, 3),
     ("high", -1, 2, 2), ("low", -1, 2, 3), ("low", 1, 2, 1), ("low", -1, 2, 1), ("low", 1, 2, 2),
     ("low", -1, 2, 2), ("high", 1, 3, 3), ("high", 1, 3, 1), ("own", 1, 4, 0), ("high", 1, 3, 2),
-    ("high", -1, 3, 3), ("low", -1, 3, 3), ("high", -1, 3, 1), ("high", -1, 3, 2), ("low", 1, 3, 3),
+    ("high", -1, 3, 3), ("high", -1, 3, 1), ("low", -1, 3, 3), ("high", -1, 3, 2), ("low", 1, 3, 3),
     ("low", -1, 3, 1), ("low", 1, 4, 3), ("low", -1, 3, 2), ("low", 1, 3, 1), ("low", 1, 4, 1),
-    ("low", 1, 3, 2), ("low", 1, 4, 2), ("high", 1, 4, 3), ("high", 1, 4, 1), ("high", 1, 4, 2),
+    ("high", 1, 4, 3), ("low", 1, 3, 2), ("high", 1, 4, 1), ("low", 1, 4, 2), ("high", 1, 4, 2),
 )
 VMEM_GRANT = 63250000
 
@@ -69,7 +70,7 @@
     s = lax.axis_index("section")
     d = lax.axis_index("dp")
     div, rem = lax.div, lax.rem
-    norms = (norms_near, norms_flat)
+    norms = (norms_flat, norms_near)
     x, zh = div(s, 2), rem(s, 2)
     y, zl, c = div(d, 8), rem(div(d, 2), NZL), rem(d, 2)
     z = zh * NZL + zl
@@ -84,8 +85,8 @@
 
     near = [dev(x, y, ring8(z, dz), rem(c + dc, 2)) for dz, dc in NEAR_STEPS]
     flat = [dev(rem(x + dx, NX), ring8(y, dy), z, c) for dx, dy in FLAT_STEPS]
-    groups = (near, flat)
-    places = (z * 2 + c, x * NY + y)
+    groups = (flat, near)
+    places = (x * NY + y, z * 2 + c)
     place_a = zl * 2 + c
     group_a = [
         (rem(zl + dz, NZL) * 2 + rem(c + dc, 2), rem(zl + dz, NZL), rem(c + dc, 2))
@@ -252,18 +253,6 @@
     high_on(block, 0)
     to_mate(block, 0, TILES)
 
-    @pl.when(s > 0)
-    def _():
-        for m in range(NY):
-            pltpu.make_async_remote_copy(
-                src_ref=part_b.at[m],
-                dst_ref=got_b.at[y],
-                send_sem=b_send,
-                recv_sem=b_recv,
-                device_id={"section": s - 1, "dp": (m * NZL + zl) * 2 + c},
-                device_id_type=MESH,
-            ).start()
-
     new_master, new_one, new_two = adam(state[0], state[3], state[1], state[2], clip)
     master_out[...] = new_master
     one_out[...] = new_one
@@ -272,7 +261,22 @@
     def source(side, k):
         return rem(y - ahead * side * k + NY, NY) * NZL
 
-    for what, side, k, j in ORDER:
+    def hand_off():
+        @pl.when(s > 0)
+        def _():
+            for m in range(NY):
+                pltpu.make_async_remote_copy(
+                    src_ref=part_b.at[m],
+                    dst_ref=got_b.at[y],
+                    send_sem=b_send,
+                    recv_sem=b_recv,
+                    device_id={"section": s - 1, "dp": (m * NZL + zl) * 2 + c},
+                    device_id_type=MESH,
+                ).start()
+
+    for turn, (what, side, k, j) in enumerate(ORDER):
+        if turn == HAND_OFF_TURN:
+            hand_off()
         b = source(side, k) + z_other(j)
         if what == "own":
             drain(tiles(b, 0, TILES), ring_recv.at[b])

time: 52.2 us -> 50.7 us (0.971)
  Pallas kernels: 51.4 us -> 50 us
    pallas_call x1, Pallas kernels: 49.2 us -> 47.8 us  [body(): pl.pallas_call(main_kernel, out_shape=(pltpu.VMEM((2, 32, HALF, WIDE), bf...]
where the time goes in v3:
time: 50.7 us; the launch traced here: 50.6 us
  Pallas kernels  50 us (99%)
  between operations  0.64 us (1%)
    pallas_call x1, Pallas kernels, body(): pl.pallas_call(main_kernel, out_shape=(pltpu.VMEM((2, 32, HALF, WIDE), bf...  47.8 us
    pallas_call x1, Pallas kernels, body(): pl.pallas_call(write_kernel, out_shape=shapes, in_specs=[vmem] * 5, out_s...  2.16 us

profile of v3, /device:TPU:1, one launch (start us, length us, event | category | flops | bytes accessed | tf_op | source)
XLA Modules:
  0.0 50.6 jit_solution(4073851026959228589)
XLA Ops:
  0.6 47.8 %update_and_gather.1 = (bf16[2,32,16,1664]{3,2,1,0:T(8,128)(2,1)S(1)}, f32[32,832]{1,0:T(8,128)S(1)}, f32[32,832]{1,0:T(8,128)S(1)}, f32[32,832]{1,0:T(8,128)S(1)}, bf16[8,32]{1,0:T(8,128)(2,1)S(1)}) custom-call(bf16[32,512]{1,0:T(8,128)(2,1)} %bitcast.11, bf16[832,512]{1,0:T(8,128)(2,1)} %bitcast.7, f32[32,832]{1,0:T(8,128)} %bitcast.8, f32[32,832]{1,0:T(8,128)} %bitcast.9, ...), custom_call_target="tpu_custom_call" | custom-call | tf_op jit(solution)/shard_map/update_and_gather/pallas_call | solution.py:353
  48.4 2.2 %write_out.1 = (bf16[1,8,32]{2,1,0:T(8,128)(2,1)}, f32[1,32,832]{2,1,0:T(8,128)}, f32[1,32,832]{2,1,0:T(8,128)}, f32[1,32,832]{2,1,0:T(8,128)}, bf16[1,32,53248]{2,1,0:T(8,128)(2,1)}) custom-call(bf16[2,32,16,1664]{3,2,1,0:T(8,128)(2,1)S(1)} %get-tuple-element.10.w, f32[32,832]{1,0:T(8,128)S(1)} %get-tuple-element.11.master, ...), custom_call_target="tpu_custom_call" | custom-call | tf_op jit(solution)/shard_map/write_out/pallas_call | solution.py:398

commit v4 on v3

--- a/solution.py
+++ b/solution.py
@@ -253,11 +253,6 @@
     high_on(block, 0)
     to_mate(block, 0, TILES)
 
-    new_master, new_one, new_two = adam(state[0], state[3], state[1], state[2], clip)
-    master_out[...] = new_master
-    one_out[...] = new_one
-    two_out[...] = new_two
-
     def source(side, k):
         return rem(y - ahead * side * k + NY, NY) * NZL
 
@@ -295,6 +290,11 @@
         else:
             drain(tiles(b, CUTS[k], TILES), z_cut_recv.at[b])
             to_mate(b, CUTS[k], TILES)
+
+    new_master, new_one, new_two = adam(state[0], state[3], state[1], state[2], clip)
+    master_out[...] = new_master
+    one_out[...] = new_one
+    two_out[...] = new_two
 
     @pl.when(s < 7)
     def _():

time: 50.7 us -> 50.7 us (level)
  no operation moved by 1% of the time
where the time goes in v4:
time: 50.7 us; the launch traced here: 50.6 us
  Pallas kernels  50 us (99%)
  between operations  0.64 us (1%)
    pallas_call x1, Pallas kernels, body(): pl.pallas_call(main_kernel, out_shape=(pltpu.VMEM((2, 32, HALF, WIDE), bf...  47.8 us
    pallas_call x1, Pallas kernels, body(): pl.pallas_call(write_kernel, out_shape=shapes, in_specs=[vmem] * 5, out_s...  2.16 us

profile of v4, /device:TPU:1, one launch (start us, length us, event | category | flops | bytes accessed | tf_op | source)
XLA Modules:
  0.0 50.6 jit_solution(8570831450355681327)
XLA Ops:
  0.6 47.8 %update_and_gather.1 = (bf16[2,32,16,1664]{3,2,1,0:T(8,128)(2,1)S(1)}, f32[32,832]{1,0:T(8,128)S(1)}, f32[32,832]{1,0:T(8,128)S(1)}, f32[32,832]{1,0:T(8,128)S(1)}, bf16[8,32]{1,0:T(8,128)(2,1)S(1)}) custom-call(bf16[32,512]{1,0:T(8,128)(2,1)} %bitcast.11, bf16[832,512]{1,0:T(8,128)(2,1)} %bitcast.7, f32[32,832]{1,0:T(8,128)} %bitcast.8, f32[32,832]{1,0:T(8,128)} %bitcast.9, ...), custom_call_target="tpu_custom_call" | custom-call | tf_op jit(solution)/shard_map/update_and_gather/pallas_call | solution.py:353
  48.4 2.2 %write_out.1 = (bf16[1,8,32]{2,1,0:T(8,128)(2,1)}, f32[1,32,832]{2,1,0:T(8,128)}, f32[1,32,832]{2,1,0:T(8,128)}, f32[1,32,832]{2,1,0:T(8,128)}, bf16[1,32,53248]{2,1,0:T(8,128)(2,1)}) custom-call(bf16[2,32,16,1664]{3,2,1,0:T(8,128)(2,1)S(1)} %get-tuple-element.10.w, f32[32,832]{1,0:T(8,128)S(1)} %get-tuple-element.11.master, ...), custom_call_target="tpu_custom_call" | custom-call | tf_op jit(solution)/shard_map/write_out/pallas_call | solution.py:398
